TPU v7x, 32 devices: a whole 2x2x4 slice. The times are simulated.
32 devices in a mesh: lon: 16 (over z, y, core), lat: 2 (over x).
Axes of the slice: x: 2, y: 2, z: 4, core: 2. Of those that a mesh axis runs over, the one named last changes fastest.
Arguments:
- field: bfloat16 [1, 64, 256, 256], P(None, 'lat', 'lon'), may hold values from -6 to 6
- depth_kernel: float32 [7, 7, 256], replicated, may hold values from -0.875 to 0.875
- layer_norm_gain: float32 [256], replicated, may hold values from 0.1 to 1.9
- inner_weight: bfloat16 [256, 1024], replicated, may hold values from -0.375 to 0.375
- outer_weight: bfloat16 [1024, 256], replicated, may hold values from -0.1875 to 0.1875
- layer_scale: float32 [256], replicated, may hold values from 0.3 to 1.5
- down_weight: bfloat16 [1024, 512], replicated, may hold values from -0.1875 to 0.1875
- cotangent: bfloat16 [1, 32, 128, 512], P(None, 'lat', 'lon'), may hold values from -6 to 6
Outputs:
- coarse: bfloat16 [1, 32, 128, 512], P(None, 'lat', 'lon')
- grad_field: bfloat16 [1, 64, 256, 256], P(None, 'lat', 'lon')
- grad_kernel: float32 [7, 7, 256], replicated
- grad_gain: float32 [256], replicated
- grad_inner: float32 [256, 1024], replicated
- grad_outer: float32 [1024, 256], replicated
- grad_scale: float32 [256], replicated
- grad_down: float32 [1024, 512], replicated
All inputs are finite; a program needn't handle non-finite values.
Results may differ from a plain program's by a relative error of at most 0.0071.
Values may be sent and summed in bfloat16 or wider, within the bound.
A program may use at most 64 MiB of HBM per device.

v0:
```python
from functools import partial
import math
import jax
import jax.numpy as jnp
from jax import lax
from jax.sharding import PartitionSpec as P

PARAMS = 1061632
EPS = 1e-06


def padded_2(cells, sides, width, closed):
    for axis, dim in sides:
        count = lax.axis_size(axis)
        ends = count if closed else count - 1
        head = lax.slice_in_dim(cells, 0, width, axis=dim)
        tail = lax.slice_in_dim(cells, cells.shape[dim] - width, cells.shape[dim], axis=dim)
        cells = jnp.concatenate(
            [
                lax.ppermute(tail, axis, [(i, (i + 1) % count) for i in range(ends)]),
                cells,
                lax.ppermute(head, axis, [((i + 1) % count, i) for i in range(ends)]),
            ],
            axis=dim,
        )
    return cells


def depth_apply(padded, kernel):
    rows = padded.shape[1] - 6
    cols = padded.shape[2] - 6
    total = jnp.zeros((padded.shape[0], rows, cols, padded.shape[3]), jnp.float32)
    for row_shift in range(7):
        for col_shift in range(7):
            total = (
                total
                + kernel[row_shift, col_shift]
                * padded[:, row_shift : row_shift + rows, col_shift : col_shift + cols]
            )
    return total


def depth_transpose(padded, kernel):
    rows = padded.shape[1] - 6
    cols = padded.shape[2] - 6
    total = jnp.zeros((padded.shape[0], rows, cols, padded.shape[3]), jnp.float32)
    for row_shift in range(7):
        for col_shift in range(7):
            total = (
                total
                + kernel[row_shift, col_shift]
                * padded[
                    :, 6 - row_shift : 6 - row_shift + rows, 6 - col_shift : 6 - col_shift + cols
                ]
            )
    return total


def kernel_terms(padded, grad):
    rows = grad.shape[1]
    cols = grad.shape[2]
    terms = []
    for row_shift in range(7):
        for col_shift in range(7):
            terms.append(
                jnp.sum(
                    padded[:, row_shift : row_shift + rows, col_shift : col_shift + cols] * grad,
                    axis=(0, 1, 2),
                )
            )
    return jnp.stack(terms).reshape(7, 7, grad.shape[3])


def to_patches(values):
    batch, rows, cols, channel_count = values.shape
    return (
        values.reshape(batch, rows // 2, 2, cols // 2, 2, channel_count)
        .transpose(0, 1, 3, 2, 4, 5)
        .reshape(-1, 4 * channel_count)
    )


def from_patches(values, shape):
    batch, rows, cols, channel_count = shape
    return (
        values.reshape(batch, rows // 2, cols // 2, 2, 2, channel_count)
        .transpose(0, 1, 3, 2, 4, 5)
        .reshape(batch, rows, cols, channel_count)
    )


def reduce_down(raw_down):
    return lax.psum(raw_down, ("lon", "lat"))


def body(
    field,
    depth_kernel,
    layer_norm_gain,
    inner_weight,
    outer_weight,
    layer_scale,
    down_weight,
    cotangent,
):
    channel_count = field.shape[3]
    wide = padded_2(field, (("lon", 2),), 3, True)
    padded = padded_2(wide, (("lat", 1),), 3, False)
    mixed = depth_apply(padded.astype(jnp.float32), depth_kernel)
    centered_input = mixed - jnp.mean(mixed, axis=-1, keepdims=True)
    inverse_deviation = lax.rsqrt(
        jnp.mean(centered_input * centered_input, axis=-1, keepdims=True) + EPS
    )
    standardized_input = centered_input * inverse_deviation
    normalized_output = (
        (standardized_input * layer_norm_gain).astype(jnp.bfloat16).reshape(-1, channel_count)
    )
    preact = jnp.dot(normalized_output, inner_weight, preferred_element_type=jnp.float32)
    hidden = jax.nn.gelu(preact, approximate=False).astype(jnp.bfloat16)
    branch = jnp.dot(hidden, outer_weight, preferred_element_type=jnp.float32)
    blocked = (field.astype(jnp.float32).reshape(-1, channel_count) + layer_scale * branch).astype(
        jnp.bfloat16
    )
    patches = to_patches(blocked.reshape(field.shape))
    coarse = jnp.dot(patches, down_weight, preferred_element_type=jnp.float32).astype(jnp.bfloat16)
    coarse = coarse.reshape(cotangent.shape)
    flat_grad = cotangent.reshape(-1, cotangent.shape[3])
    raw_down = jnp.dot(patches.T, flat_grad, preferred_element_type=jnp.float32)
    grad_patch = jnp.dot(flat_grad, down_weight.T, preferred_element_type=jnp.float32).astype(
        jnp.bfloat16
    )
    grad_blocked = from_patches(grad_patch, field.shape).reshape(-1, channel_count)
    raw_scale = jnp.sum(grad_blocked.astype(jnp.float32) * branch, axis=0)
    grad_branch = (grad_blocked.astype(jnp.float32) * layer_scale).astype(jnp.bfloat16)
    grad_hidden = jnp.dot(grad_branch, outer_weight.T, preferred_element_type=jnp.float32)
    grad_pre = jax.vjp(partial(jax.nn.gelu, approximate=False), preact)[1](grad_hidden)[0].astype(
        jnp.bfloat16
    )
    raw_outer = jnp.dot(hidden.T, grad_branch, preferred_element_type=jnp.float32)
    raw_inner = jnp.dot(normalized_output.T, grad_pre, preferred_element_type=jnp.float32)
    normalized_gradient = jnp.dot(
        grad_pre, inner_weight.T, preferred_element_type=jnp.float32
    ).reshape(mixed.shape)
    unclipped_gain = jnp.sum(normalized_gradient * standardized_input, axis=(0, 1, 2))
    gain_scaled_output = normalized_gradient * layer_norm_gain
    depthwise_gradient = (
        gain_scaled_output
        - jnp.mean(gain_scaled_output, axis=-1, keepdims=True)
        - standardized_input
        * jnp.mean(gain_scaled_output * standardized_input, axis=-1, keepdims=True)
    ) * inverse_deviation
    depthwise_gradient = depthwise_gradient.astype(jnp.bfloat16)
    grad_wide = padded_2(depthwise_gradient, (("lon", 2),), 3, True)
    grad_padded = padded_2(grad_wide, (("lat", 1),), 3, False).astype(jnp.float32)
    spread = depth_transpose(grad_padded, depth_kernel)
    grad_field = (grad_blocked.reshape(field.shape).astype(jnp.float32) + spread).astype(
        jnp.bfloat16
    )
    raw_kernel = kernel_terms(padded.astype(jnp.float32), depthwise_gradient.astype(jnp.float32))
    summed_down = reduce_down(raw_down)
    limit = math.sqrt(PARAMS)
    sum_kernel, sum_gain, sum_inner, sum_outer, sum_scale = lax.psum(
        (raw_kernel, unclipped_gain, raw_inner, raw_outer, raw_scale), ("lon", "lat")
    )
    total = (
        jnp.sum(sum_kernel * sum_kernel)
        + jnp.sum(sum_gain * sum_gain)
        + jnp.sum(sum_inner * sum_inner)
        + jnp.sum(sum_outer * sum_outer)
        + jnp.sum(sum_scale * sum_scale)
        + jnp.sum(summed_down * summed_down)
    )
    factor = jnp.minimum(1.0, limit / jnp.sqrt(total + EPS))
    grad_kernel = sum_kernel * factor
    grad_gain = sum_gain * factor
    grad_inner = sum_inner * factor
    grad_outer = sum_outer * factor
    grad_scale = sum_scale * factor
    grad_down = summed_down * factor
    return (
        coarse,
        grad_field,
        grad_kernel,
        grad_gain,
        grad_inner,
        grad_outer,
        grad_scale,
        grad_down,
    )


def solution(mesh):
    return jax.shard_map(
        body,
        mesh=mesh,
        in_specs=(
            P(None, "lat", "lon", None),
            P(),
            P(),
            P(),
            P(),
            P(),
            P(),
            P(None, "lat", "lon", None),
        ),
        out_specs=(
            P(None, "lat", "lon", None),
            P(None, "lat", "lon", None),
            P(),
            P(),
            P(),
            P(),
            P(),
            P(),
        ),
        check_vma=False,
    )
```

profile of v0, /device:TPU:0, one launch (start us, length us, event | category | flops | bytes accessed | tf_op | source)
XLA Modules:
  0.0 220.6 jit_solution(751683770909935926)
XLA Ops:
  7.2 1.1 fusion.114
  8.8 5.1 %collective-permute-start.1 = (bf16[1,32,3,256]{3,2,1,0:T(4,128)(2,1)S(1)}, bf16[1,32,3,256]{3,2,1,0:T(4,128)(2,1)S(1)}, u32[]{:S(2)}, u32[]{:S(2)}) collective-permute-start(bf16[1,32,3,256]{3,2,1,0:T(4,128)(2,1)S(1)} %get-tuple-element.79), channel_id=1, source_target_pairs={{2,0},{4,2},{6,4},{8,6},{10,8},{12,10},{14,12},{16,14},{18,16},{20... | collective-permute-start | bytes 147464 | tf_op jit(solution)/shard_map/ppermute | solution.py:22
  13.9 1.0 fusion.115
  15.1 1.4 convolution_convert_fusion
  16.5 1.0 fusion.116
  17.8 0.8 pad_maximum_fusion.5
  18.6 3.8 %collective-permute-start.2 = (bf16[1,3,22,256]{3,2,1,0:T(8,128)(2,1)S(1)}, bf16[1,3,22,256]{3,2,1,0:T(8,128)(2,1)S(1)}, u32[]{:S(2)}, u32[]{:S(2)}) collective-permute-start(bf16[1,3,22,256]{3,2,1,0:T(8,128)(2,1)S(1)} %get-tuple-element.74), channel_id=1, source_target_pairs={{0,1},{2,3},{4,5},{6,7},{8,9},{10,11},{12,13},{14,15},{16,17},{18,... | collective-permute-start | bytes 101384 | tf_op jit(solution)/shard_map/ppermute | solution.py:20
  22.4 1.3 collective-permute-start.3
  23.7 1.5 fusion.117
  25.8 1.2 reshape.366
  26.9 1.3 collective-permute-done.3
  28.8 4.5 %fusion.112 = (f32[32,16]{1,0:T(8,128)S(1)}, f32[1,32,16,256]{3,2,1,0:T(8,128)S(1)}) fusion(f32[1,38,22,256]{3,2,1,0:T(8,128)S(1)} %maximum_convert_fusion, f32[256]{0:T(256)} %bitcast.49, f32[256]{0:T(256)} %bitcast.48, f32[256]{0:T(256)S(1)} %bitcast.144, f32[256]{0:T(256)S(1)} %bitcast.146, f32[256]{0:T(256)S(1)} %bitcast.148, f32[256]{0:T(256)S(1)} %bitcast.150, ...), kind=kLoop, calls=%fused_computation.259 | loop fusion | flops 12844544 | bytes 26266624 | tf_op jit(solution)/shard_map/reduce_sum | solution.py:110
  34.3 5.8 %multiply_convert_fusion = (bf16[512,1024]{1,0:T(8,128)(2,1)S(1)}, f32[512,1024]{1,0:T(8,128)S(1)}, f32[512,1024]{1,0:T(8,128)S(1)}) fusion(bf16[512,256]{1,0:T(8,128)(2,1)S(1)} %bitcast.138, bf16[256,1024]{1,0:T(8,128)(2,1)S(1)} %copy-done.98), kind=kOutput, calls=%fused_computation.53 | convolution fusion | flops 302514176 | bytes 6029312 | tf_op jit(solution)/shard_map/dot_general | solution.py:118
  40.1 1.5 fusion.110
  41.6 1.0 multiply_reduce_fusion.3
  42.6 1.0 add_convert_fusion
  43.6 1.1 multiply_reduce_fusion.6
  44.8 1.4 fusion.118
  46.3 0.9 copy.22
  47.2 1.1 reshape.359
  48.4 0.7 broadcast_multiply_fusion.6
  49.0 0.7 div.20
  49.7 1.6 multiply_reduce_fusion.4
  51.3 3.0 %fusion.54 = (f32[256]{0:T(256)}, f32[256]{0:T(256)}, f32[256]{0:T(256)}, f32[256]{0:T(256)}, f32[256]{0:T(256)}, /*index=5*/f32[256]{0:T(256)}, f32[256]{0:T(25...) fusion(f32[1,38,22,256]{3,2,1,0:T(8,128)S(1)} %maximum_convert_, ...), kind=kLoop, calls=%fused_computation.120 | loop fusion | flops 5893632 | bytes 10775552 | tf_op jit(solution)/shard_map/reduce_sum | solution.py:66
  54.3 1.1 fusion.55
  55.4 1.8 fusion.107
  57.2 0.7 fusion.53
  58.3 2.9 %stack.199 = f32[49,256]{1,0:T(8,128)S(1)} concatenate(f32[1,256]{1,0:T(1,128)S(1)} %bitcast.250, f32[1,256]{1,0:T(1,128)S(1)} %bitcast.252, f32[1,256]{1,0:T(1,128)S(1)} %bitcast.253, f32[1,256]{1,0:T(1,128)S(1)} %bitcast.254, f32[1,256]{1,0:T(1,128)S(1)} %bitcast.255, f32[1,256]{1,0:T(1,128)S(1)} %bitcast.256, f32[1,256]{1,0:T(1,128)S(1)} %bitcast.257, f32[1,256]{1,0:T(1,128)S(1)} %bitcast.258, ...), dimensions={0} | concatenate | bytes 100352 | tf_op jit(solution)/shard_map/stack | solution.py:71
  61.4 4.4 %collective-permute-start.5 = (bf16[1,32,3,256]{3,2,1,0:T(4,128)(2,1)S(1)}, bf16[1,32,3,256]{3,2,1,0:T(4,128)(2,1)S(1)}, u32[]{:S(2)}, u32[]{:S(2)}) collective-permute-start(bf16[1,32,3,256]{3,2,1,0:T(4,128)(2,1)S(1)} %get-tuple-element.77), channel_id=1, source_target_pairs={{2,0},{4,2},{6,4},{8,6},{10,8},{12,10},{14,12},{16,14},{18,16},{20... | collective-permute-start | bytes 147464 | tf_op jit(solution)/shard_map/ppermute | solution.py:22
  65.8 38.1 %all-reduce = (f32[7,7,256]{2,1,0:T(8,128)S(1)}, f32[256]{0:T(256)S(1)}, f32[256]{0:T(256)S(1)}) all-reduce(f32[7,7,256]{2,1,0:T(8,128)S(1)} %reshape.363, f32[256]{0:T(256)} %get-tuple-element.57, f32[256]{0:T(256)} %get-tuple-element.70), channel_id=1, replica_groups=mesh['lon'=16,'lat'=2] {'lon','lat'}, use_global_device_ids=true, to_apply=%region_53.0 | all-reduce | flops 13056 | bytes 104448 | tf_op jit(solution)/shard_map/psum | solution.py:162
  104.0 1.0 fusion.6
  105.0 0.6 multiply_reduce_fusion.8
  105.6 4.2 %collective-permute-start.6 = (bf16[1,3,22,256]{3,2,1,0:T(8,128)(2,1)S(1)}, bf16[1,3,22,256]{3,2,1,0:T(8,128)(2,1)S(1)}, u32[]{:S(2)}, u32[]{:S(2)}) collective-permute-start(bf16[1,3,22,256]{3,2,1,0:T(8,128)(2,1)S(1)} %get-tuple-element.72), channel_id=1, source_target_pairs={{0,1},{2,3},{4,5},{6,7},{8,9},{10,11},{12,13},{14,15},{16,17},{18,... | collective-permute-start | bytes 101384 | tf_op jit(solution)/shard_map/ppermute | solution.py:20
  109.8 1.3 collective-permute-start.7
  111.1 0.7 multiply_reduce_fusion.9
  113.0 2.6 %collective-permute-done.7 = bf16[1,3,22,256]{3,2,1,0:T(8,128)(2,1)S(1)} collective-permute-done((bf16[1,3,22,256]{3,2,1,0:T(8,128)(2,1)S(1)}, bf16[1,3,22,256]{3,2,1,0:T(8,128)(2,1)S(1)}, u32[]{:S(2)}, u32[]{:S(2)}) %collective-permute-start.7) | collective-permute-done | bytes 33824 | tf_op jit(solution)/shard_map/ppermute | solution.py:22
  116.2 5.1 %fusion.58 = bf16[1,32,16,256]{3,2,1,0:T(8,128)(2,1)} fusion(f32[1,32,16,256]{3,2,1,0:T(8,128)S(1)} %copy-done.7, f32[1,38,22,256]{3,2,1,0:T(8,128)S(1)} %maximum_convert_fusion.1, f32[256]{0:T(256)} %bitcast.49, f32[256]{0:T(256)} %bitcast.48, f32[256]{0:T(256)S(1)} %bitcast.145, f32[256]{0:T(256)S(1)} %bitcast.147, f32[256]{0:T(256)S(1)} %bitcast.149, ...), kind=kLoop, calls=%fused_computation.125 | loop fusion | flops 12976128 | bytes 26526720 | tf_op jit(solution)/shard_map/convert_element_type | solution.py:156
  121.3 79.2 %all-reduce.4.cloned.1.call-done = (f32[256,1024]{1,0:T(8,128)}, f32[1024,256]{1,0:T(8,128)}, f32[1024,512]{1,0:T(8,128)}) async-done(((f32[256,1024]{1,0:T(8,128)}, f32[1024,256]{1,0:T(8,128)}, f32[1024,512]{1,0:T(8,128)}), (f32[256,1024]{1,0:T(8,128)}, f32[1024,256]{1,0:T(8,128)}, f32[1024,512]{1,0:T(8,128)})) %all-reduce.4.cloned.1.call-update) | async-done | bytes 4194320 | tf_op jit(solution)/shard_map/psum | solution.py:162
  200.5 2.9 %multiply_reduce_fusion = f32[]{:T(128)} fusion(f32[1024,512]{1,0:T(8,128)} %get-tuple-element.64), kind=kLoop, calls=%fused_computation.51 | loop fusion | flops 1048575 | bytes 2097156 | tf_op jit(solution)/shard_map/reduce_sum | solution.py:171
  203.3 0.9 multiply_reduce_fusion.1
  204.2 0.9 multiply_reduce_fusion.2
  207.8 0.6 broadcast_multiply_fusion.7
  208.3 1.5 broadcast_multiply_fusion
  209.9 1.0 broadcast_multiply_fusion.1
  210.9 0.6 copy-done.3
  211.5 1.1 broadcast_multiply_fusion.2
  212.6 0.6 broadcast_multiply_fusion.8
  213.1 0.6 broadcast_multiply_fusion.3
  (220 shorter events, 3.0 us)
Async XLA Ops:
  7.2 193.3 %all-reduce.4.cloned.1.call-start = ((), (), s32[]{:S(2)}) async-start(), calls=%async_computation | async-start | bytes 8388608 | tf_op jit(solution)/shard_map/psum | solution.py:162
  8.3 9.4 %collective-permute-start = (bf16[1,32,3,256]{3,2,1,0:T(4,128)(2,1)S(1)}, bf16[1,32,3,256]{3,2,1,0:T(4,128)(2,1)S(1)}, u32[]{:S(2)}, u32[]{:S(2)}) collective-permute-start(bf16[1,32,3,256]{3,2,1,0:T(4,128)(2,1)S(1)} %get-tuple-element.78), channel_id=1, source_target_pairs={{0,2},{2,4},{4,6},{6,8},{8,10},{10,12},{12,14},{14,16},{16,18},{18... | collective-permute-start | bytes 147464 | tf_op jit(solution)/shard_map/ppermute | solution.py:20
  8.8 8.9 %collective-permute-start.1 = (bf16[1,32,3,256]{3,2,1,0:T(4,128)(2,1)S(1)}, bf16[1,32,3,256]{3,2,1,0:T(4,128)(2,1)S(1)}, u32[]{:S(2)}, u32[]{:S(2)}) collective-permute-start(bf16[1,32,3,256]{3,2,1,0:T(4,128)(2,1)S(1)} %get-tuple-element.79), channel_id=1, source_target_pairs={{2,0},{4,2},{6,4},{8,6},{10,8},{12,10},{14,12},{16,14},{18,16},{20... | collective-permute-start | bytes 147464 | tf_op jit(solution)/shard_map/ppermute | solution.py:22
  18.6 8.4 %collective-permute-start.2 = (bf16[1,3,22,256]{3,2,1,0:T(8,128)(2,1)S(1)}, bf16[1,3,22,256]{3,2,1,0:T(8,128)(2,1)S(1)}, u32[]{:S(2)}, u32[]{:S(2)}) collective-permute-start(bf16[1,3,22,256]{3,2,1,0:T(8,128)(2,1)S(1)} %get-tuple-element.74), channel_id=1, source_target_pairs={{0,1},{2,3},{4,5},{6,7},{8,9},{10,11},{12,13},{14,15},{16,17},{18,... | collective-permute-start | bytes 101384 | tf_op jit(solution)/shard_map/ppermute | solution.py:20
  22.4 5.9 %collective-permute-start.3 = (bf16[1,3,22,256]{3,2,1,0:T(8,128)(2,1)S(1)}, bf16[1,3,22,256]{3,2,1,0:T(8,128)(2,1)S(1)}, u32[]{:S(2)}, u32[]{:S(2)}) collective-permute-start(bf16[1,3,22,256]{3,2,1,0:T(8,128)(2,1)S(1)} %get-tuple-element.75), channel_id=1, source_target_pairs={{1,0},{3,2},{5,4},{7,6},{9,8},{11,10},{13,12},{15,14},{17,16},{19,... | collective-permute-start | bytes 101384 | tf_op jit(solution)/shard_map/ppermute | solution.py:22
  57.9 57.9 %copy-start.16 = (f32[1,1,256]{2,1,0:T(1,128)S(1)}, f32[1,1,256]{2,1,0:T(1,128)}, u32[]{:S(2)}) copy-start(f32[1,1,256]{2,1,0:T(1,128)} %copy-done.15) | copy-start | bytes 3076
  57.9 57.9 %copy-start.18 = (f32[1,1,256]{2,1,0:T(1,128)S(1)}, f32[1,1,256]{2,1,0:T(1,128)}, u32[]{:S(2)}) copy-start(f32[1,1,256]{2,1,0:T(1,128)} %copy-done.17) | copy-start | bytes 3076
  57.9 57.9 %copy-start.20 = (f32[1,1,256]{2,1,0:T(1,128)S(1)}, f32[1,1,256]{2,1,0:T(1,128)}, u32[]{:S(2)}) copy-start(f32[1,1,256]{2,1,0:T(1,128)} %copy-done.19) | copy-start | bytes 3076
  58.0 57.9 %copy-start.22 = (f32[1,1,256]{2,1,0:T(1,128)S(1)}, f32[1,1,256]{2,1,0:T(1,128)}, u32[]{:S(2)}) copy-start(f32[1,1,256]{2,1,0:T(1,128)} %copy-done.21) | copy-start | bytes 3076
  58.0 57.9 %copy-start.24 = (f32[1,1,256]{2,1,0:T(1,128)S(1)}, f32[1,1,256]{2,1,0:T(1,128)}, u32[]{:S(2)}) copy-start(f32[1,1,256]{2,1,0:T(1,128)} %copy-done.23) | copy-start | bytes 3076
  58.0 57.9 %copy-start.26 = (f32[1,1,256]{2,1,0:T(1,128)S(1)}, f32[1,1,256]{2,1,0:T(1,128)}, u32[]{:S(2)}) copy-start(f32[1,1,256]{2,1,0:T(1,128)} %copy-done.25) | copy-start | bytes 3076
  58.0 57.9 %copy-start.28 = (f32[1,1,256]{2,1,0:T(1,128)S(1)}, f32[1,1,256]{2,1,0:T(1,128)}, u32[]{:S(2)}) copy-start(f32[1,1,256]{2,1,0:T(1,128)} %copy-done.27) | copy-start | bytes 3076
  58.0 57.9 %copy-start.30 = (f32[1,1,256]{2,1,0:T(1,128)S(1)}, f32[1,1,256]{2,1,0:T(1,128)}, u32[]{:S(2)}) copy-start(f32[1,1,256]{2,1,0:T(1,128)} %copy-done.29) | copy-start | bytes 3076
  58.0 57.9 %copy-start.32 = (f32[1,1,256]{2,1,0:T(1,128)S(1)}, f32[1,1,256]{2,1,0:T(1,128)}, u32[]{:S(2)}) copy-start(f32[1,1,256]{2,1,0:T(1,128)} %copy-done.31) | copy-start | bytes 3076
  58.0 57.9 %copy-start.34 = (f32[1,1,256]{2,1,0:T(1,128)S(1)}, f32[1,1,256]{2,1,0:T(1,128)}, u32[]{:S(2)}) copy-start(f32[1,1,256]{2,1,0:T(1,128)} %copy-done.33) | copy-start | bytes 3076
  58.0 57.9 %copy-start.36 = (f32[1,1,256]{2,1,0:T(1,128)S(1)}, f32[1,1,256]{2,1,0:T(1,128)}, u32[]{:S(2)}) copy-start(f32[1,1,256]{2,1,0:T(1,128)} %copy-done.35) | copy-start | bytes 3076
  58.0 57.9 %copy-start.38 = (f32[1,1,256]{2,1,0:T(1,128)S(1)}, f32[1,1,256]{2,1,0:T(1,128)}, u32[]{:S(2)}) copy-start(f32[1,1,256]{2,1,0:T(1,128)} %copy-done.37) | copy-start | bytes 3076
  58.0 57.9 %copy-start.40 = (f32[1,1,256]{2,1,0:T(1,128)S(1)}, f32[1,1,256]{2,1,0:T(1,128)}, u32[]{:S(2)}) copy-start(f32[1,1,256]{2,1,0:T(1,128)} %copy-done.39) | copy-start | bytes 3076
  58.1 57.9 %copy-start.42 = (f32[1,1,256]{2,1,0:T(1,128)S(1)}, f32[1,1,256]{2,1,0:T(1,128)}, u32[]{:S(2)}) copy-start(f32[1,1,256]{2,1,0:T(1,128)} %copy-done.41) | copy-start | bytes 3076
  58.1 57.9 %copy-start.44 = (f32[1,1,256]{2,1,0:T(1,128)S(1)}, f32[1,1,256]{2,1,0:T(1,128)}, u32[]{:S(2)}) copy-start(f32[1,1,256]{2,1,0:T(1,128)} %copy-done.43) | copy-start | bytes 3076
  58.1 57.9 %copy-start.46 = (f32[1,1,256]{2,1,0:T(1,128)S(1)}, f32[1,1,256]{2,1,0:T(1,128)}, u32[]{:S(2)}) copy-start(f32[1,1,256]{2,1,0:T(1,128)} %copy-done.45) | copy-start | bytes 3076
  58.1 57.9 %copy-start.48 = (f32[1,1,256]{2,1,0:T(1,128)S(1)}, f32[1,1,256]{2,1,0:T(1,128)}, u32[]{:S(2)}) copy-start(f32[1,1,256]{2,1,0:T(1,128)} %copy-done.47) | copy-start | bytes 3076
  58.1 57.9 %copy-start.50 = (f32[1,1,256]{2,1,0:T(1,128)S(1)}, f32[1,1,256]{2,1,0:T(1,128)}, u32[]{:S(2)}) copy-start(f32[1,1,256]{2,1,0:T(1,128)} %copy-done.49) | copy-start | bytes 3076
  58.1 57.9 %copy-start.52 = (f32[1,1,256]{2,1,0:T(1,128)S(1)}, f32[1,1,256]{2,1,0:T(1,128)}, u32[]{:S(2)}) copy-start(f32[1,1,256]{2,1,0:T(1,128)} %copy-done.51) | copy-start | bytes 3076
  58.1 57.9 %copy-start.54 = (f32[1,1,256]{2,1,0:T(1,128)S(1)}, f32[1,1,256]{2,1,0:T(1,128)}, u32[]{:S(2)}) copy-start(f32[1,1,256]{2,1,0:T(1,128)} %copy-done.53) | copy-start | bytes 3076
  58.1 57.9 %copy-start.56 = (f32[1,1,256]{2,1,0:T(1,128)S(1)}, f32[1,1,256]{2,1,0:T(1,128)}, u32[]{:S(2)}) copy-start(f32[1,1,256]{2,1,0:T(1,128)} %copy-done.55) | copy-start | bytes 3076
  58.1 57.9 %copy-start.58 = (f32[1,1,256]{2,1,0:T(1,128)S(1)}, f32[1,1,256]{2,1,0:T(1,128)}, u32[]{:S(2)}) copy-start(f32[1,1,256]{2,1,0:T(1,128)} %copy-done.57) | copy-start | bytes 3076
  58.1 57.9 %copy-start.60 = (f32[1,1,256]{2,1,0:T(1,128)S(1)}, f32[1,1,256]{2,1,0:T(1,128)}, u32[]{:S(2)}) copy-start(f32[1,1,256]{2,1,0:T(1,128)} %copy-done.59) | copy-start | bytes 3076
  58.2 57.9 %copy-start.62 = (f32[1,1,256]{2,1,0:T(1,128)S(1)}, f32[1,1,256]{2,1,0:T(1,128)}, u32[]{:S(2)}) copy-start(f32[1,1,256]{2,1,0:T(1,128)} %copy-done.61) | copy-start | bytes 3076
  58.2 57.9 %copy-start.64 = (f32[1,1,256]{2,1,0:T(1,128)S(1)}, f32[1,1,256]{2,1,0:T(1,128)}, u32[]{:S(2)}) copy-start(f32[1,1,256]{2,1,0:T(1,128)} %copy-done.63) | copy-start | bytes 3076
  58.2 57.9 %copy-start.66 = (f32[1,1,256]{2,1,0:T(1,128)S(1)}, f32[1,1,256]{2,1,0:T(1,128)}, u32[]{:S(2)}) copy-start(f32[1,1,256]{2,1,0:T(1,128)} %copy-done.65) | copy-start | bytes 3076
  58.2 57.9 %copy-start.68 = (f32[1,1,256]{2,1,0:T(1,128)S(1)}, f32[1,1,256]{2,1,0:T(1,128)}, u32[]{:S(2)}) copy-start(f32[1,1,256]{2,1,0:T(1,128)} %copy-done.67) | copy-start | bytes 3076
  58.2 57.9 %copy-start.70 = (f32[1,1,256]{2,1,0:T(1,128)S(1)}, f32[1,1,256]{2,1,0:T(1,128)}, u32[]{:S(2)}) copy-start(f32[1,1,256]{2,1,0:T(1,128)} %copy-done.69) | copy-start | bytes 3076
  58.2 57.9 %copy-start.72 = (f32[1,1,256]{2,1,0:T(1,128)S(1)}, f32[1,1,256]{2,1,0:T(1,128)}, u32[]{:S(2)}) copy-start(f32[1,1,256]{2,1,0:T(1,128)} %copy-done.71) | copy-start | bytes 3076
  58.2 57.9 %copy-start.74 = (f32[1,1,256]{2,1,0:T(1,128)S(1)}, f32[1,1,256]{2,1,0:T(1,128)}, u32[]{:S(2)}) copy-start(f32[1,1,256]{2,1,0:T(1,128)} %copy-done.73) | copy-start | bytes 3076
  58.2 57.9 %copy-start.76 = (f32[1,1,256]{2,1,0:T(1,128)S(1)}, f32[1,1,256]{2,1,0:T(1,128)}, u32[]{:S(2)}) copy-start(f32[1,1,256]{2,1,0:T(1,128)} %copy-done.75) | copy-start | bytes 3076
  58.2 57.9 %copy-start.78 = (f32[1,1,256]{2,1,0:T(1,128)S(1)}, f32[1,1,256]{2,1,0:T(1,128)}, u32[]{:S(2)}) copy-start(f32[1,1,256]{2,1,0:T(1,128)} %copy-done.77) | copy-start | bytes 3076
  58.2 57.9 %copy-start.80 = (f32[1,1,256]{2,1,0:T(1,128)S(1)}, f32[1,1,256]{2,1,0:T(1,128)}, u32[]{:S(2)}) copy-start(f32[1,1,256]{2,1,0:T(1,128)} %copy-done.79) | copy-start | bytes 3076
  58.3 57.9 %copy-start.82 = (f32[1,1,256]{2,1,0:T(1,128)S(1)}, f32[1,1,256]{2,1,0:T(1,128)}, u32[]{:S(2)}) copy-start(f32[1,1,256]{2,1,0:T(1,128)} %copy-done.81) | copy-start | bytes 3076
  58.3 57.9 %copy-start.84 = (f32[1,1,256]{2,1,0:T(1,128)S(1)}, f32[1,1,256]{2,1,0:T(1,128)}, u32[]{:S(2)}) copy-start(f32[1,1,256]{2,1,0:T(1,128)} %copy-done.83) | copy-start | bytes 3076
  58.3 57.9 %copy-start.86 = (f32[1,1,256]{2,1,0:T(1,128)S(1)}, f32[1,1,256]{2,1,0:T(1,128)}, u32[]{:S(2)}) copy-start(f32[1,1,256]{2,1,0:T(1,128)} %copy-done.85) | copy-start | bytes 3076
  58.3 57.9 %copy-start.88 = (f32[1,1,256]{2,1,0:T(1,128)S(1)}, f32[1,1,256]{2,1,0:T(1,128)}, u32[]{:S(2)}) copy-start(f32[1,1,256]{2,1,0:T(1,128)} %copy-done.87) | copy-start | bytes 3076
  58.3 57.9 %copy-start.90 = (f32[1,1,256]{2,1,0:T(1,128)S(1)}, f32[1,1,256]{2,1,0:T(1,128)}, u32[]{:S(2)}) copy-start(f32[1,1,256]{2,1,0:T(1,128)} %copy-done.89) | copy-start | bytes 3076
  58.3 57.9 %copy-start.92 = (f32[1,1,256]{2,1,0:T(1,128)S(1)}, f32[1,1,256]{2,1,0:T(1,128)}, u32[]{:S(2)}) copy-start(f32[1,1,256]{2,1,0:T(1,128)} %copy-done.91) | copy-start | bytes 3076
  61.3 44.3 %collective-permute-start.4 = (bf16[1,32,3,256]{3,2,1,0:T(4,128)(2,1)S(1)}, bf16[1,32,3,256]{3,2,1,0:T(4,128)(2,1)S(1)}, u32[]{:S(2)}, u32[]{:S(2)}) collective-permute-start(bf16[1,32,3,256]{3,2,1,0:T(4,128)(2,1)S(1)} %get-tuple-element.76), channel_id=1, source_target_pairs={{0,2},{2,4},{4,6},{6,8},{8,10},{10,12},{12,14},{14,16},{16,18},{18... | collective-permute-start | bytes 147464 | tf_op jit(solution)/shard_map/ppermute | solution.py:20
  61.4 44.2 %collective-permute-start.5 = (bf16[1,32,3,256]{3,2,1,0:T(4,128)(2,1)S(1)}, bf16[1,32,3,256]{3,2,1,0:T(4,128)(2,1)S(1)}, u32[]{:S(2)}, u32[]{:S(2)}) collective-permute-start(bf16[1,32,3,256]{3,2,1,0:T(4,128)(2,1)S(1)} %get-tuple-element.77), channel_id=1, source_target_pairs={{2,0},{4,2},{6,4},{8,6},{10,8},{12,10},{14,12},{16,14},{18,16},{20... | collective-permute-start | bytes 147464 | tf_op jit(solution)/shard_map/ppermute | solution.py:22
  105.6 7.4 %collective-permute-start.6 = (bf16[1,3,22,256]{3,2,1,0:T(8,128)(2,1)S(1)}, bf16[1,3,22,256]{3,2,1,0:T(8,128)(2,1)S(1)}, u32[]{:S(2)}, u32[]{:S(2)}) collective-permute-start(bf16[1,3,22,256]{3,2,1,0:T(8,128)(2,1)S(1)} %get-tuple-element.72), channel_id=1, source_target_pairs={{0,1},{2,3},{4,5},{6,7},{8,9},{10,11},{12,13},{14,15},{16,17},{18,... | collective-permute-start | bytes 101384 | tf_op jit(solution)/shard_map/ppermute | solution.py:20
  109.8 5.9 %collective-permute-start.7 = (bf16[1,3,22,256]{3,2,1,0:T(8,128)(2,1)S(1)}, bf16[1,3,22,256]{3,2,1,0:T(8,128)(2,1)S(1)}, u32[]{:S(2)}, u32[]{:S(2)}) collective-permute-start(bf16[1,3,22,256]{3,2,1,0:T(8,128)(2,1)S(1)} %get-tuple-element.73), channel_id=1, source_target_pairs={{1,0},{3,2},{5,4},{7,6},{9,8},{11,10},{13,12},{15,14},{17,16},{19,... | collective-permute-start | bytes 101384 | tf_op jit(solution)/shard_map/ppermute | solution.py:22
  (60 other events, 651.4 us)
Sparse Core Ops, SparseCore 0:
  57.3 143.0 all-reduce.3
where the time goes:
time: 221 us
  waiting for transfers between devices  83.1 us (38%)
  blocking collectives  38.1 us (17%)
  other arithmetic  29.6 us (13%)
  starting transfers between devices  20.6 us (9%)
  between operations  19.6 us (9%)
  matrix products  16.1 us (7%)
  local copies, waits for them, and re-layouts  13.5 us (6%)
    psum x1, waiting for transfers between devices, body(): lax.psum((raw_kernel, unclipped_gain, raw_inner, raw_outer, raw_scale), (...  79.2 us
    psum x1, blocking collectives, body(): lax.psum((raw_kernel, unclipped_gain, raw_inner, raw_outer, raw_scale), (...  38.1 us
    ppermute x4, starting transfers between devices, padded_2(): lax.ppermute(head, axis, [((i + 1) % count, i) for i in range(ends)])  12.1 us
    ppermute x4, starting transfers between devices, padded_2(): lax.ppermute(tail, axis, [(i, (i + 1) % count) for i in range(ends)])  8.5 us
    dot_general x1, matrix products, body(): jnp.dot(normalized_output, inner_weight, preferred_element_type=jnp.float32)  5.79 us
    convert_element_type x1, other arithmetic, body(): (grad_blocked.reshape(field.shape).astype(jnp.float32) + spread).astype(j...  5.07 us
    reduce_sum x3, other arithmetic, kernel_terms(): jnp.sum(padded[:, row_shift:row_shift + rows, col_shift:col_shift + cols]...  4.77 us
    reduce_sum x1, other arithmetic, body(): centered_input = mixed - jnp.mean(mixed, axis=-1, keepdims=True)  4.53 us
  transfers between devices with their start and end apart: 9, of which 3 were waited for; matrix products, arithmetic and copies ran while one was open for 8% of the time, Pallas kernels for 0%

commit v1 on v0

--- a/solution.py
+++ b/solution.py
@@ -159,8 +159,9 @@
     raw_kernel = kernel_terms(padded.astype(jnp.float32), depthwise_gradient.astype(jnp.float32))
     summed_down = reduce_down(raw_down)
     limit = math.sqrt(PARAMS)
-    sum_kernel, sum_gain, sum_inner, sum_outer, sum_scale = lax.psum(
-        (raw_kernel, unclipped_gain, raw_inner, raw_outer, raw_scale), ("lon", "lat")
+    lots_all_rest = lambda block_in: jax.lax.psum(jax.lax.psum(block_in, "lat"), "lon")
+    sum_kernel, sum_gain, sum_inner, sum_outer, sum_scale = lots_all_rest(
+        (raw_kernel, unclipped_gain, raw_inner, raw_outer, raw_scale)
     )
     total = (
         jnp.sum(sum_kernel * sum_kernel)

time: 221 us -> 369 us (1.67)
  waiting for transfers between devices: 83.1 us -> 203 us
  blocking collectives: 38.1 us -> 67.9 us
    psum x1 -> x3, waiting for transfers between devices: 79.2 us -> 199 us  [the longest x1 101 us: reduce_down(): return lax.psum(raw_down, ('lon', 'lat'))]
    psum x1 -> x2, blocking collectives: 38.1 us -> 67.9 us  [the longest x1 57.8 us: body(): jax.lax.psum(jax.lax.psum(block_in, 'lat'), 'lon')]
  transfers between devices with their start and end apart: 9 -> 11, of which waited for: 3 -> 4; matrix products, arithmetic and copies ran while one was open for 8% -> 8% of each run, Pallas kernels for 0% -> 0%
where the time goes in v1:
time: 369 us; the launch traced here: 368 us
  waiting for transfers between devices  203 us (55%)
  blocking collectives  67.9 us (18%)
  other arithmetic  32 us (9%)
  between operations  19.5 us (5%)
  starting transfers between devices  19.4 us (5%)
  matrix products  15.5 us (4%)
  local copies, waits for them, and re-layouts  11 us (3%)
    psum x1, waiting for transfers between devices, reduce_down(): return lax.psum(raw_down, ('lon', 'lat'))  101 us
    psum x1, waiting for transfers between devices, body(): jax.lax.psum(jax.lax.psum(block_in, 'lat'), 'lon')  97.9 us
    psum x1, blocking collectives, body(): jax.lax.psum(jax.lax.psum(block_in, 'lat'), 'lon')  57.8 us
    ppermute x4, starting transfers between devices, padded_2(): lax.ppermute(head, axis, [((i + 1) % count, i) for i in range(ends)])  12.1 us
    psum x1, blocking collectives, body(): jax.lax.psum(block_in, 'lat')  10 us
  transfers between devices with their start and end apart: 11, of which 4 were waited for; matrix products, arithmetic and copies ran while one was open for 8% of the time, Pallas kernels for 0%

profile of v1, /device:TPU:0, one launch (start us, length us, event | category | flops | bytes accessed | tf_op | source)
XLA Modules:
  0.0 368.4 jit_solution(1904691904731222047)
XLA Ops:
  7.2 1.1 fusion.114
  8.8 5.1 %collective-permute-start.1 = (bf16[1,32,3,256]{3,2,1,0:T(4,128)(2,1)S(1)}, bf16[1,32,3,256]{3,2,1,0:T(4,128)(2,1)S(1)}, u32[]{:S(2)}, u32[]{:S(2)}) collective-permute-start(bf16[1,32,3,256]{3,2,1,0:T(4,128)(2,1)S(1)} %get-tuple-element.83), channel_id=1, source_target_pairs={{2,0},{4,2},{6,4},{8,6},{10,8},{12,10},{14,12},{16,14},{18,16},{20... | collective-permute-start | bytes 147464 | tf_op jit(solution)/shard_map/ppermute | solution.py:22
  13.9 1.0 fusion.115
  15.1 1.4 convolution_convert_fusion
  16.5 1.0 fusion.116
  17.8 0.8 pad_maximum_fusion.5
  18.6 3.8 %collective-permute-start.2 = (bf16[1,3,22,256]{3,2,1,0:T(8,128)(2,1)S(1)}, bf16[1,3,22,256]{3,2,1,0:T(8,128)(2,1)S(1)}, u32[]{:S(2)}, u32[]{:S(2)}) collective-permute-start(bf16[1,3,22,256]{3,2,1,0:T(8,128)(2,1)S(1)} %get-tuple-element.78), channel_id=1, source_target_pairs={{0,1},{2,3},{4,5},{6,7},{8,9},{10,11},{12,13},{14,15},{16,17},{18,... | collective-permute-start | bytes 101384 | tf_op jit(solution)/shard_map/ppermute | solution.py:20
  22.4 1.3 collective-permute-start.3
  23.7 1.5 fusion.117
  25.8 1.2 reshape.366
  26.9 1.3 collective-permute-done.3
  28.8 4.5 %fusion.112 = (f32[32,16]{1,0:T(8,128)S(1)}, f32[1,32,16,256]{3,2,1,0:T(8,128)S(1)}) fusion(f32[1,38,22,256]{3,2,1,0:T(8,128)S(1)} %maximum_convert_fusion, f32[256]{0:T(256)} %bitcast.49, f32[256]{0:T(256)} %bitcast.48, f32[256]{0:T(256)S(1)} %bitcast.144, f32[256]{0:T(256)S(1)} %bitcast.146, f32[256]{0:T(256)S(1)} %bitcast.148, f32[256]{0:T(256)S(1)} %bitcast.150, ...), kind=kLoop, calls=%fused_computation.259 | loop fusion | flops 12844544 | bytes 26266624 | tf_op jit(solution)/shard_map/reduce_sum | solution.py:110
  34.3 5.8 %multiply_convert_fusion = (bf16[512,1024]{1,0:T(8,128)(2,1)S(1)}, f32[512,1024]{1,0:T(8,128)S(1)}, f32[512,1024]{1,0:T(8,128)S(1)}) fusion(bf16[512,256]{1,0:T(8,128)(2,1)S(1)} %bitcast.138, bf16[256,1024]{1,0:T(8,128)(2,1)S(1)} %copy-done.114), kind=kOutput, calls=%fused_computation.53 | convolution fusion | flops 302514176 | bytes 6029312 | tf_op jit(solution)/shard_map/dot_general | solution.py:118
  40.1 1.5 fusion.110
  41.6 1.0 multiply_reduce_fusion.3
  42.6 1.0 add_convert_fusion
  43.6 0.6 multiply_reduce_fusion.6
  44.2 1.4 fusion.118
  45.9 0.6 broadcast_multiply_fusion.6
  46.6 0.9 copy.22
  47.5 1.1 reshape.359
  48.6 1.4 div.20
  50.0 1.6 multiply_reduce_fusion.4
  51.6 3.0 fusion.54
  54.6 0.7 fusion.53
  55.5 1.1 fusion.55
  56.9 1.8 fusion.107
  58.9 4.4 %collective-permute-start.5 = (bf16[1,32,3,256]{3,2,1,0:T(4,128)(2,1)S(1)}, bf16[1,32,3,256]{3,2,1,0:T(4,128)(2,1)S(1)}, u32[]{:S(2)}, u32[]{:S(2)}) collective-permute-start(bf16[1,32,3,256]{3,2,1,0:T(4,128)(2,1)S(1)} %get-tuple-element.81), channel_id=1, source_target_pairs={{2,0},{4,2},{6,4},{8,6},{10,8},{12,10},{14,12},{16,14},{18,16},{20... | collective-permute-start | bytes 147464 | tf_op jit(solution)/shard_map/ppermute | solution.py:22
  63.3 10.0 %all-reduce.2 = (f32[7,7,256]{2,1,0:T(8,128)S(1)}, f32[256]{0:T(256)S(1)}, f32[256]{0:T(256)S(1)}) all-reduce(f32[7,7,256]{2,1,0:T(8,128)S(1)} %reshape.363, f32[256]{0:T(256)S(1)} %copy-done.109, f32[256]{0:T(256)S(1)} %copy-done.108), channel_id=1, replica_groups=mesh['lon'=16,'lat'=2] {'lat'}, use_global_device_ids=true, to_apply=%region_53.0 | all-reduce | flops 13056 | bytes 104448 | tf_op jit(solution)/shard_map/psum | solution.py:162
  73.4 57.8 %all-reduce = (f32[7,7,256]{2,1,0:T(8,128)S(1)}, f32[256]{0:T(256)S(1)}, f32[256]{0:T(256)S(1)}) all-reduce(f32[7,7,256]{2,1,0:T(8,128)S(1)} %get-tuple-element.64, f32[256]{0:T(256)S(1)} %get-tuple-element.65, f32[256]{0:T(256)S(1)} %get-tuple-element.66), channel_id=1, replica_groups=mesh['lon'=16,'lat'=2] {'lon'}, use_global_device_ids=true, to_apply=%region_54.0 | all-reduce | flops 13056 | bytes 104448 | tf_op jit(solution)/shard_map/psum | solution.py:162
  131.2 0.6 multiply_reduce_fusion.8
  131.8 1.0 fusion.6
  133.2 0.7 multiply_reduce_fusion.9
  133.9 2.7 collective-permute-start.6
  136.6 1.3 collective-permute-start.7
  137.9 0.6 multiply_reduce_fusion.10
  139.8 2.6 collective-permute-done.7
  143.1 5.1 %fusion.58 = bf16[1,32,16,256]{3,2,1,0:T(8,128)(2,1)} fusion(f32[1,32,16,256]{3,2,1,0:T(8,128)S(1)} %copy-done.5, f32[1,38,22,256]{3,2,1,0:T(8,128)S(1)} %maximum_convert_fusion.1, f32[256]{0:T(256)} %bitcast.49, f32[256]{0:T(256)} %bitcast.48, f32[256]{0:T(256)S(1)} %bitcast.145, f32[256]{0:T(256)S(1)} %bitcast.147, f32[256]{0:T(256)S(1)} %bitcast.149, ...), kind=kLoop, calls=%fused_computation.125 | loop fusion | flops 12976128 | bytes 26526720 | tf_op jit(solution)/shard_map/convert_element_type | solution.py:156
  148.2 101.3 %all-reduce.8.cloned.1.call-done = f32[1024,512]{1,0:T(8,128)} async-done(((f32[1024,512]{1,0:T(8,128)}), f32[1024,512]{1,0:T(8,128)}) %all-reduce.8.cloned.1.call-update) | async-done | bytes 2097168 | tf_op jit(solution)/shard_map/psum | solution.py:93
  249.5 2.7 multiply_reduce_fusion
  252.2 97.9 %all-reduce.10.cloned.1.call-done = (f32[256,1024]{1,0:T(8,128)}, f32[1024,256]{1,0:T(8,128)}) async-done(((f32[256,1024]{1,0:T(8,128)}, f32[1024,256]{1,0:T(8,128)}), (f32[256,1024]{1,0:T(8,128)}, f32[1024,256]{1,0:T(8,128)})) %all-reduce.10.cloned.1.call-update) | async-done | bytes 2097168 | tf_op jit(solution)/shard_map/psum | solution.py:162
  350.1 2.2 multiply_reduce_fusion.1
  352.3 2.1 multiply_reduce_fusion.2
  357.1 1.0 broadcast_multiply_fusion.1
  358.1 1.0 broadcast_multiply_fusion.2
  359.2 0.6 broadcast_multiply_fusion.3
  359.8 0.6 broadcast_multiply_fusion.7
  360.4 1.5 broadcast_multiply_fusion
  (259 shorter events, 3.6 us)
Async XLA Ops:
  7.2 135.5 %all-reduce.12.cloned.1.call-start = ((), (), s32[]{:S(2)}) async-start(), calls=%async_computation.2 | async-start | bytes 4194304 | tf_op jit(solution)/shard_map/psum | solution.py:162
  8.3 9.4 %collective-permute-start = (bf16[1,32,3,256]{3,2,1,0:T(4,128)(2,1)S(1)}, bf16[1,32,3,256]{3,2,1,0:T(4,128)(2,1)S(1)}, u32[]{:S(2)}, u32[]{:S(2)}) collective-permute-start(bf16[1,32,3,256]{3,2,1,0:T(4,128)(2,1)S(1)} %get-tuple-element.82), channel_id=1, source_target_pairs={{0,2},{2,4},{4,6},{6,8},{8,10},{10,12},{12,14},{14,16},{16,18},{18... | collective-permute-start | bytes 147464 | tf_op jit(solution)/shard_map/ppermute | solution.py:20
  8.8 8.9 %collective-permute-start.1 = (bf16[1,32,3,256]{3,2,1,0:T(4,128)(2,1)S(1)}, bf16[1,32,3,256]{3,2,1,0:T(4,128)(2,1)S(1)}, u32[]{:S(2)}, u32[]{:S(2)}) collective-permute-start(bf16[1,32,3,256]{3,2,1,0:T(4,128)(2,1)S(1)} %get-tuple-element.83), channel_id=1, source_target_pairs={{2,0},{4,2},{6,4},{8,6},{10,8},{12,10},{14,12},{16,14},{18,16},{20... | collective-permute-start | bytes 147464 | tf_op jit(solution)/shard_map/ppermute | solution.py:22
  14.9 13.5 %copy-start.11 = (f32[1,1,256]{2,1,0:T(1,128)}, f32[1,1,256]{2,1,0:T(1,128)S(1)}, u32[]{:S(2)}) copy-start(f32[1,1,256]{2,1,0:T(1,128)S(1)} %get-tuple-element.84) | copy-start | bytes 3076
  14.9 13.5 %copy-start.13 = (f32[1,1,256]{2,1,0:T(1,128)}, f32[1,1,256]{2,1,0:T(1,128)S(1)}, u32[]{:S(2)}) copy-start(f32[1,1,256]{2,1,0:T(1,128)S(1)} %get-tuple-element.85) | copy-start | bytes 3076
  14.9 13.5 %copy-start.15 = (f32[1,1,256]{2,1,0:T(1,128)}, f32[1,1,256]{2,1,0:T(1,128)S(1)}, u32[]{:S(2)}) copy-start(f32[1,1,256]{2,1,0:T(1,128)S(1)} %get-tuple-element.86) | copy-start | bytes 3076
  14.9 13.5 %copy-start.17 = (f32[1,1,256]{2,1,0:T(1,128)}, f32[1,1,256]{2,1,0:T(1,128)S(1)}, u32[]{:S(2)}) copy-start(f32[1,1,256]{2,1,0:T(1,128)S(1)} %get-tuple-element.87) | copy-start | bytes 3076
  14.9 13.5 %copy-start.19 = (f32[1,1,256]{2,1,0:T(1,128)}, f32[1,1,256]{2,1,0:T(1,128)S(1)}, u32[]{:S(2)}) copy-start(f32[1,1,256]{2,1,0:T(1,128)S(1)} %get-tuple-element.88) | copy-start | bytes 3076
  14.9 13.5 %copy-start.21 = (f32[1,1,256]{2,1,0:T(1,128)}, f32[1,1,256]{2,1,0:T(1,128)S(1)}, u32[]{:S(2)}) copy-start(f32[1,1,256]{2,1,0:T(1,128)S(1)} %get-tuple-element.89) | copy-start | bytes 3076
  15.0 13.5 %copy-start.23 = (f32[1,1,256]{2,1,0:T(1,128)}, f32[1,1,256]{2,1,0:T(1,128)S(1)}, u32[]{:S(2)}) copy-start(f32[1,1,256]{2,1,0:T(1,128)S(1)} %get-tuple-element.90) | copy-start | bytes 3076
  15.0 13.5 %copy-start.25 = (f32[1,1,256]{2,1,0:T(1,128)}, f32[1,1,256]{2,1,0:T(1,128)S(1)}, u32[]{:S(2)}) copy-start(f32[1,1,256]{2,1,0:T(1,128)S(1)} %get-tuple-element.91) | copy-start | bytes 3076
  15.0 13.5 %copy-start.27 = (f32[1,1,256]{2,1,0:T(1,128)}, f32[1,1,256]{2,1,0:T(1,128)S(1)}, u32[]{:S(2)}) copy-start(f32[1,1,256]{2,1,0:T(1,128)S(1)} %get-tuple-element.92) | copy-start | bytes 3076
  15.0 13.5 %copy-start.29 = (f32[1,1,256]{2,1,0:T(1,128)}, f32[1,1,256]{2,1,0:T(1,128)S(1)}, u32[]{:S(2)}) copy-start(f32[1,1,256]{2,1,0:T(1,128)S(1)} %get-tuple-element.93) | copy-start | bytes 3076
  15.0 13.5 %copy-start.31 = (f32[1,1,256]{2,1,0:T(1,128)}, f32[1,1,256]{2,1,0:T(1,128)S(1)}, u32[]{:S(2)}) copy-start(f32[1,1,256]{2,1,0:T(1,128)S(1)} %get-tuple-element.94) | copy-start | bytes 3076
  15.0 13.5 %copy-start.33 = (f32[1,1,256]{2,1,0:T(1,128)}, f32[1,1,256]{2,1,0:T(1,128)S(1)}, u32[]{:S(2)}) copy-start(f32[1,1,256]{2,1,0:T(1,128)S(1)} %get-tuple-element.95) | copy-start | bytes 3076
  15.0 13.5 %copy-start.35 = (f32[1,1,256]{2,1,0:T(1,128)}, f32[1,1,256]{2,1,0:T(1,128)S(1)}, u32[]{:S(2)}) copy-start(f32[1,1,256]{2,1,0:T(1,128)S(1)} %get-tuple-element.96) | copy-start | bytes 3076
  15.0 13.5 %copy-start.37 = (f32[1,1,256]{2,1,0:T(1,128)}, f32[1,1,256]{2,1,0:T(1,128)S(1)}, u32[]{:S(2)}) copy-start(f32[1,1,256]{2,1,0:T(1,128)S(1)} %get-tuple-element.97) | copy-start | bytes 3076
  15.0 13.5 %copy-start.39 = (f32[1,1,256]{2,1,0:T(1,128)}, f32[1,1,256]{2,1,0:T(1,128)S(1)}, u32[]{:S(2)}) copy-start(f32[1,1,256]{2,1,0:T(1,128)S(1)} %get-tuple-element.98) | copy-start | bytes 3076
  15.0 13.5 %copy-start.41 = (f32[1,1,256]{2,1,0:T(1,128)}, f32[1,1,256]{2,1,0:T(1,128)S(1)}, u32[]{:S(2)}) copy-start(f32[1,1,256]{2,1,0:T(1,128)S(1)} %get-tuple-element.99) | copy-start | bytes 3076
  15.1 13.5 %copy-start.43 = (f32[1,1,256]{2,1,0:T(1,128)}, f32[1,1,256]{2,1,0:T(1,128)S(1)}, u32[]{:S(2)}) copy-start(f32[1,1,256]{2,1,0:T(1,128)S(1)} %get-tuple-element.100) | copy-start | bytes 3076
  15.1 13.5 %copy-start.45 = (f32[1,1,256]{2,1,0:T(1,128)}, f32[1,1,256]{2,1,0:T(1,128)S(1)}, u32[]{:S(2)}) copy-start(f32[1,1,256]{2,1,0:T(1,128)S(1)} %get-tuple-element.101) | copy-start | bytes 3076
  15.1 13.5 %copy-start.47 = (f32[1,1,256]{2,1,0:T(1,128)}, f32[1,1,256]{2,1,0:T(1,128)S(1)}, u32[]{:S(2)}) copy-start(f32[1,1,256]{2,1,0:T(1,128)S(1)} %get-tuple-element.102) | copy-start | bytes 3076
  15.1 13.1 %copy-start.4 = (bf16[1,32,16,256]{3,2,1,0:T(8,128)(2,1)S(1)}, bf16[1,32,16,256]{3,2,1,0:T(8,128)(2,1)}, u32[]{:S(2)}) copy-start(bf16[1,32,16,256]{3,2,1,0:T(8,128)(2,1)} %param.8) | copy-start | bytes 786436
  17.6 11.0 %copy-start.49 = (f32[1,1,256]{2,1,0:T(1,128)}, f32[1,1,256]{2,1,0:T(1,128)S(1)}, u32[]{:S(2)}) copy-start(f32[1,1,256]{2,1,0:T(1,128)S(1)} %get-tuple-element.103) | copy-start | bytes 3076
  17.6 11.0 %copy-start.51 = (f32[1,1,256]{2,1,0:T(1,128)}, f32[1,1,256]{2,1,0:T(1,128)S(1)}, u32[]{:S(2)}) copy-start(f32[1,1,256]{2,1,0:T(1,128)S(1)} %get-tuple-element.104) | copy-start | bytes 3076
  17.6 11.0 %copy-start.53 = (f32[1,1,256]{2,1,0:T(1,128)}, f32[1,1,256]{2,1,0:T(1,128)S(1)}, u32[]{:S(2)}) copy-start(f32[1,1,256]{2,1,0:T(1,128)S(1)} %get-tuple-element.105) | copy-start | bytes 3076
  17.6 11.0 %copy-start.55 = (f32[1,1,256]{2,1,0:T(1,128)}, f32[1,1,256]{2,1,0:T(1,128)S(1)}, u32[]{:S(2)}) copy-start(f32[1,1,256]{2,1,0:T(1,128)S(1)} %get-tuple-element.106) | copy-start | bytes 3076
  17.6 11.0 %copy-start.57 = (f32[1,1,256]{2,1,0:T(1,128)}, f32[1,1,256]{2,1,0:T(1,128)S(1)}, u32[]{:S(2)}) copy-start(f32[1,1,256]{2,1,0:T(1,128)S(1)} %get-tuple-element.107) | copy-start | bytes 3076
  17.6 11.0 %copy-start.59 = (f32[1,1,256]{2,1,0:T(1,128)}, f32[1,1,256]{2,1,0:T(1,128)S(1)}, u32[]{:S(2)}) copy-start(f32[1,1,256]{2,1,0:T(1,128)S(1)} %get-tuple-element.108) | copy-start | bytes 3076
  17.6 11.0 %copy-start.61 = (f32[1,1,256]{2,1,0:T(1,128)}, f32[1,1,256]{2,1,0:T(1,128)S(1)}, u32[]{:S(2)}) copy-start(f32[1,1,256]{2,1,0:T(1,128)S(1)} %get-tuple-element.109) | copy-start | bytes 3076
  17.6 11.0 %copy-start.63 = (f32[1,1,256]{2,1,0:T(1,128)}, f32[1,1,256]{2,1,0:T(1,128)S(1)}, u32[]{:S(2)}) copy-start(f32[1,1,256]{2,1,0:T(1,128)S(1)} %get-tuple-element.110) | copy-start | bytes 3076
  17.6 11.0 %copy-start.65 = (f32[1,1,256]{2,1,0:T(1,128)}, f32[1,1,256]{2,1,0:T(1,128)S(1)}, u32[]{:S(2)}) copy-start(f32[1,1,256]{2,1,0:T(1,128)S(1)} %get-tuple-element.111) | copy-start | bytes 3076
  17.6 11.0 %copy-start.67 = (f32[1,1,256]{2,1,0:T(1,128)}, f32[1,1,256]{2,1,0:T(1,128)S(1)}, u32[]{:S(2)}) copy-start(f32[1,1,256]{2,1,0:T(1,128)S(1)} %get-tuple-element.112) | copy-start | bytes 3076
  17.7 11.0 %copy-start.69 = (f32[1,1,256]{2,1,0:T(1,128)}, f32[1,1,256]{2,1,0:T(1,128)S(1)}, u32[]{:S(2)}) copy-start(f32[1,1,256]{2,1,0:T(1,128)S(1)} %get-tuple-element.113) | copy-start | bytes 3076
  17.7 11.0 %copy-start.71 = (f32[1,1,256]{2,1,0:T(1,128)}, f32[1,1,256]{2,1,0:T(1,128)S(1)}, u32[]{:S(2)}) copy-start(f32[1,1,256]{2,1,0:T(1,128)S(1)} %get-tuple-element.114) | copy-start | bytes 3076
  17.7 11.0 %copy-start.73 = (f32[1,1,256]{2,1,0:T(1,128)}, f32[1,1,256]{2,1,0:T(1,128)S(1)}, u32[]{:S(2)}) copy-start(f32[1,1,256]{2,1,0:T(1,128)S(1)} %get-tuple-element.115) | copy-start | bytes 3076
  17.7 11.0 %copy-start.75 = (f32[1,1,256]{2,1,0:T(1,128)}, f32[1,1,256]{2,1,0:T(1,128)S(1)}, u32[]{:S(2)}) copy-start(f32[1,1,256]{2,1,0:T(1,128)S(1)} %get-tuple-element.116) | copy-start | bytes 3076
  17.7 11.0 %copy-start.77 = (f32[1,1,256]{2,1,0:T(1,128)}, f32[1,1,256]{2,1,0:T(1,128)S(1)}, u32[]{:S(2)}) copy-start(f32[1,1,256]{2,1,0:T(1,128)S(1)} %get-tuple-element.117) | copy-start | bytes 3076
  17.7 11.0 %copy-start.79 = (f32[1,1,256]{2,1,0:T(1,128)}, f32[1,1,256]{2,1,0:T(1,128)S(1)}, u32[]{:S(2)}) copy-start(f32[1,1,256]{2,1,0:T(1,128)S(1)} %get-tuple-element.118) | copy-start | bytes 3076
  17.7 11.0 %copy-start.81 = (f32[1,1,256]{2,1,0:T(1,128)}, f32[1,1,256]{2,1,0:T(1,128)S(1)}, u32[]{:S(2)}) copy-start(f32[1,1,256]{2,1,0:T(1,128)S(1)} %get-tuple-element.119) | copy-start | bytes 3076
  18.6 8.4 %collective-permute-start.2 = (bf16[1,3,22,256]{3,2,1,0:T(8,128)(2,1)S(1)}, bf16[1,3,22,256]{3,2,1,0:T(8,128)(2,1)S(1)}, u32[]{:S(2)}, u32[]{:S(2)}) collective-permute-start(bf16[1,3,22,256]{3,2,1,0:T(8,128)(2,1)S(1)} %get-tuple-element.78), channel_id=1, source_target_pairs={{0,1},{2,3},{4,5},{6,7},{8,9},{10,11},{12,13},{14,15},{16,17},{18,... | collective-permute-start | bytes 101384 | tf_op jit(solution)/shard_map/ppermute | solution.py:20
  22.4 5.9 %collective-permute-start.3 = (bf16[1,3,22,256]{3,2,1,0:T(8,128)(2,1)S(1)}, bf16[1,3,22,256]{3,2,1,0:T(8,128)(2,1)S(1)}, u32[]{:S(2)}, u32[]{:S(2)}) collective-permute-start(bf16[1,3,22,256]{3,2,1,0:T(8,128)(2,1)S(1)} %get-tuple-element.79), channel_id=1, source_target_pairs={{1,0},{3,2},{5,4},{7,6},{9,8},{11,10},{13,12},{15,14},{17,16},{19,... | collective-permute-start | bytes 101384 | tf_op jit(solution)/shard_map/ppermute | solution.py:22
  45.7 203.8 %all-reduce.8.cloned.1.call-start = ((), (), s32[]{:S(2)}) async-start(), calls=%async_computation | async-start | bytes 4194304 | tf_op jit(solution)/shard_map/psum | solution.py:93
  58.7 291.3 %all-reduce.10.cloned.1.call-start = ((), (), s32[]{:S(2)}) async-start(), calls=%async_computation.1 | async-start | bytes 4194304 | tf_op jit(solution)/shard_map/psum | solution.py:162
  58.8 75.0 %collective-permute-start.4 = (bf16[1,32,3,256]{3,2,1,0:T(4,128)(2,1)S(1)}, bf16[1,32,3,256]{3,2,1,0:T(4,128)(2,1)S(1)}, u32[]{:S(2)}, u32[]{:S(2)}) collective-permute-start(bf16[1,32,3,256]{3,2,1,0:T(4,128)(2,1)S(1)} %get-tuple-element.80), channel_id=1, source_target_pairs={{0,2},{2,4},{4,6},{6,8},{8,10},{10,12},{12,14},{14,16},{16,18},{18... | collective-permute-start | bytes 147464 | tf_op jit(solution)/shard_map/ppermute | solution.py:20
  58.9 74.9 %collective-permute-start.5 = (bf16[1,32,3,256]{3,2,1,0:T(4,128)(2,1)S(1)}, bf16[1,32,3,256]{3,2,1,0:T(4,128)(2,1)S(1)}, u32[]{:S(2)}, u32[]{:S(2)}) collective-permute-start(bf16[1,32,3,256]{3,2,1,0:T(4,128)(2,1)S(1)} %get-tuple-element.81), channel_id=1, source_target_pairs={{2,0},{4,2},{6,4},{8,6},{10,8},{12,10},{14,12},{16,14},{18,16},{20... | collective-permute-start | bytes 147464 | tf_op jit(solution)/shard_map/ppermute | solution.py:22
  133.9 5.9 %collective-permute-start.6 = (bf16[1,3,22,256]{3,2,1,0:T(8,128)(2,1)S(1)}, bf16[1,3,22,256]{3,2,1,0:T(8,128)(2,1)S(1)}, u32[]{:S(2)}, u32[]{:S(2)}) collective-permute-start(bf16[1,3,22,256]{3,2,1,0:T(8,128)(2,1)S(1)} %get-tuple-element.76), channel_id=1, source_target_pairs={{0,1},{2,3},{4,5},{6,7},{8,9},{10,11},{12,13},{14,15},{16,17},{18,... | collective-permute-start | bytes 101384 | tf_op jit(solution)/shard_map/ppermute | solution.py:20
  136.6 5.9 %collective-permute-start.7 = (bf16[1,3,22,256]{3,2,1,0:T(8,128)(2,1)S(1)}, bf16[1,3,22,256]{3,2,1,0:T(8,128)(2,1)S(1)}, u32[]{:S(2)}, u32[]{:S(2)}) collective-permute-start(bf16[1,3,22,256]{3,2,1,0:T(8,128)(2,1)S(1)} %get-tuple-element.77), channel_id=1, source_target_pairs={{1,0},{3,2},{5,4},{7,6},{9,8},{11,10},{13,12},{15,14},{17,16},{19,... | collective-permute-start | bytes 101384 | tf_op jit(solution)/shard_map/ppermute | solution.py:22
  (78 other events, 521.0 us)
Sparse Core Ops, SparseCore 0:
  45.8 63.0 all-reduce.11
  115.7 133.7 all-reduce.7
  253.1 96.9 all-reduce.9
